TPU v7x, 32 devices: a whole 2x2x4 slice. The times are simulated.
32 devices in a mesh: rep: 8 (over z, x), shard: 4 (over y, core).
Axes of the slice: x: 2, y: 2, z: 4, core: 2. Of those that a mesh axis runs over, the one named last changes fastest.
Arguments:
- tokens: bfloat16 [16384, 1024], P(('rep', 'shard')), may hold values from -6 to 6
- positions: int32 [16384], P(('rep', 'shard')), may hold values from 0 to 511, as said below
- lengths: int32 [64], replicated, may hold values from 0 to 512, as said below
- owner: int32 [64], replicated, may hold values from 0 to 31, as said below
- qkv_weight: bfloat16 [1024, 3072], P('shard'), may hold values from -0.1875 to 0.1875
- out_weight: bfloat16 [1024, 1024], P('shard'), may hold values from -1.5 to 1.5
- in_weight: bfloat16 [1024, 4096], P('shard'), may hold values from -0.1875 to 0.1875
- in_bias: bfloat16 [4096], P('shard'), may hold values from -3 to 3
- fc_weight: bfloat16 [4096, 1024], P('shard'), may hold values from -0.09375 to 0.09375
- fc_bias: bfloat16 [1024], P('shard'), may hold values from -3 to 3
- norm_gain: bfloat16 [1024], P('shard'), may hold values from 0.25 to 1.75
- norm_bias: bfloat16 [1024], P('shard'), may hold values from -2 to 2
- cotangent: bfloat16 [16384, 1024], P(('rep', 'shard')), may hold values from -6 to 6
Outputs:
- layer_out: bfloat16 [16384, 1024], P(('rep', 'shard'))
- input_grad: bfloat16 [16384, 1024], P(('rep', 'shard'))
- grad_qkv: float32 [1024, 3072], P('shard')
- grad_out: float32 [1024, 1024], P('shard')
- grad_in: float32 [1024, 4096], P('shard')
- grad_in_bias: float32 [4096], P('shard')
- grad_fc: float32 [4096, 1024], P('shard')
- grad_fc_bias: float32 [1024], P('shard')
- grad_gain: float32 [1024], P('shard')
- grad_norm_bias: float32 [1024], P('shard')
Inputs may be any that keep to these rules, and one draw needn't show every extreme that they name: Sequences 2 i and 2 i + 1 go to one device; their lengths sum to at most 512; some sequence has exactly 512 tokens; a length may be 0. Sequences 2 i and 2 i + 1 have the same owner, and every device owns exactly one such pair. `positions`: a token's position within its sequence, with the sequences packed as the steps say; unused slots hold 0.
All inputs are finite; a program needn't handle non-finite values.
Results may differ from a plain program's by a relative error of at most 0.011.
Values may be sent and summed in bfloat16 or wider, within the bound.
A program may use at most 256 MiB of HBM per device.

v0:
```python
from functools import partial
import math
import jax
import jax.numpy as jnp
from jax import lax
from jax.sharding import PartitionSpec as P

D = 1024
HEADS = 16
HEAD_DIM = 64
ROT_DIM = 32
TOK_DEV = 512
EPS = 1e-05
NEG = -1000000000.0
SCORE_SCALE = 0.125


def layout(lengths, owner, device):
    owned_mask = (owner == device).astype(jnp.int32)
    seq_ends = jnp.cumsum(lengths * owned_mask)
    seq_load = jnp.sum(lengths * owned_mask)
    slot_index = jnp.arange(TOK_DEV, dtype=jnp.int32)
    passed = (seq_ends[None, :] <= slot_index[:, None]) & (owned_mask[None, :] > 0)
    segment = jnp.sum(passed.astype(jnp.int32), axis=1)
    in_use = slot_index < seq_load
    return (jnp.where(in_use, segment, TOK_DEV + slot_index), in_use)


def layer_norm(inputs, scale_gain, norm_shift):
    center = inputs - jnp.mean(inputs, axis=-1, keepdims=True)
    spread = jnp.mean(center * center, axis=-1, keepdims=True)
    return center * lax.rsqrt(spread + EPS) * scale_gain + norm_shift


def rotary_tables(positions):
    freq_index = jnp.arange(ROT_DIM // 2, dtype=jnp.float32)
    inverse = jnp.exp(freq_index * (-2.0 * math.log(10000.0) / ROT_DIM))
    angles = positions.astype(jnp.float32)[:, None] * inverse[None, :]
    return (jnp.cos(angles), jnp.sin(angles))


def rotate(field, cosine, sine_table):
    row_count = field.shape[0]
    head_count = field.shape[1]
    turned = field[..., :ROT_DIM].reshape(row_count, head_count, ROT_DIM // 2, 2)
    first_half = turned[..., 0]
    second_half = turned[..., 1]
    cos_wide = cosine[:, None, :]
    sin_wide = sine_table[:, None, :]
    joined = jnp.stack(
        [
            first_half * cos_wide - second_half * sin_wide,
            second_half * cos_wide + first_half * sin_wide,
        ],
        -1,
    )
    return jnp.concatenate(
        [joined.reshape(row_count, head_count, ROT_DIM), field[..., ROT_DIM:]], -1
    )


def block_scores(query_block, key_block, allowed_block):
    raw_scores = (
        jnp.einsum("qhd,khd->hqk", query_block, key_block, preferred_element_type=jnp.float32)
        * SCORE_SCALE
    )
    return jnp.where(allowed_block[None], raw_scores, NEG)


def attend(queries, key_rows, value_rows, allowed):
    row_count = queries.shape[0]
    head_count = queries.shape[1]
    block_rows = min(512, row_count)
    group_size = min(8, head_count)
    head_parts = []
    norm_parts = []
    for head_start in range(0, head_count, group_size):
        head_end = head_start + group_size
        scores = block_scores(
            queries[0:block_rows, head_start:head_end], key_rows[:, head_start:head_end], allowed
        )
        row_peak = jnp.max(scores, axis=-1, keepdims=True)
        exponent = jnp.exp(scores - row_peak)
        row_total = jnp.sum(exponent, axis=-1, keepdims=True)
        soft_weights = (exponent / row_total).astype(jnp.bfloat16)
        row_parts = jnp.einsum(
            "hqk,khd->qhd",
            soft_weights,
            value_rows[:, head_start:head_end],
            preferred_element_type=jnp.float32,
        )
        row_norms = (row_peak + jnp.log(row_total))[..., 0]
        head_parts.append(row_parts)
        norm_parts.append(row_norms)
    return (jnp.concatenate(head_parts, 1), jnp.concatenate(norm_parts, 0))


def attend_back(queries, key_rows, value_rows, grad_attended, log_norm, allowed):
    row_count = queries.shape[0]
    head_count = queries.shape[1]
    block_rows = min(512, row_count)
    group_size = min(8, head_count)
    query_parts = []
    key_parts = []
    value_parts = []
    for head_start in range(0, head_count, group_size):
        head_end = head_start + group_size
        key_block = key_rows[:, head_start:head_end]
        value_block = value_rows[:, head_start:head_end]
        query_block = queries[0:block_rows, head_start:head_end]
        grad_block = grad_attended[0:block_rows, head_start:head_end]
        scores = block_scores(query_block, key_block, allowed)
        soft_full = jnp.exp(scores - log_norm[head_start:head_end, 0:block_rows][..., None])
        soft_low = soft_full.astype(jnp.bfloat16)
        grad_soft = jnp.einsum(
            "qhd,khd->hqk", grad_block, value_block, preferred_element_type=jnp.float32
        )
        row_delta = jnp.sum(soft_full * grad_soft, axis=-1, keepdims=True)
        grad_scores = (soft_full * (grad_soft - row_delta)).astype(jnp.bfloat16)
        row_parts = (
            jnp.einsum("hqk,khd->qhd", grad_scores, key_block, preferred_element_type=jnp.float32)
            * SCORE_SCALE
        )
        key_sum = (
            jnp.einsum("hqk,qhd->khd", grad_scores, query_block, preferred_element_type=jnp.float32)
            * SCORE_SCALE
        )
        value_sum = jnp.einsum(
            "hqk,qhd->khd", soft_low, grad_block, preferred_element_type=jnp.float32
        )
        query_parts.append(row_parts)
        key_parts.append(key_sum)
        value_parts.append(value_sum)
    return (
        jnp.concatenate(query_parts, 1),
        jnp.concatenate(key_parts, 1),
        jnp.concatenate(value_parts, 1),
    )


def body(
    tokens,
    positions,
    lengths,
    owner,
    qkv_weight,
    out_weight,
    in_weight,
    in_bias,
    fc_weight,
    fc_bias,
    norm_gain,
    norm_bias,
    cotangent,
):
    device = lax.axis_index(("rep", "shard"))
    segment, in_use = layout(lengths, owner, device)
    row_count = tokens.shape[0]
    slot_index = jnp.arange(row_count, dtype=jnp.int32)
    allowed = (segment[:, None] == segment[None, :]) & (slot_index[None, :] <= slot_index[:, None])
    gathered = (
        lax.all_gather(qkv_weight, "shard", axis=0, tiled=True),
        lax.all_gather(out_weight, "shard", axis=0, tiled=True),
        lax.all_gather(in_weight, "shard", axis=0, tiled=True),
        lax.all_gather(in_bias, "shard", axis=0, tiled=True),
        lax.all_gather(fc_weight, "shard", axis=0, tiled=True),
        lax.all_gather(fc_bias, "shard", axis=0, tiled=True),
        lax.all_gather(norm_gain, "shard", axis=0, tiled=True),
        lax.all_gather(norm_bias, "shard", axis=0, tiled=True),
    )
    qkv_full, out_full, in_full, in_bias_full, fc_full, fc_bias_full, gain_full, shift_full = (
        gathered
    )
    inputs = tokens.astype(jnp.float32)
    normed = layer_norm(
        inputs, gain_full.astype(jnp.float32), shift_full.astype(jnp.float32)
    ).astype(jnp.bfloat16)
    merged_rows = jnp.dot(normed, qkv_full, preferred_element_type=jnp.float32)
    cosine, sine_table = rotary_tables(positions)
    queries = rotate(
        merged_rows[:, :D].reshape(row_count, HEADS, HEAD_DIM), cosine, sine_table
    ).astype(jnp.bfloat16)
    key_rows = rotate(
        merged_rows[:, D : 2 * D].reshape(row_count, HEADS, HEAD_DIM), cosine, sine_table
    ).astype(jnp.bfloat16)
    value_rows = merged_rows[:, 2 * D :].reshape(row_count, HEADS, HEAD_DIM).astype(jnp.bfloat16)
    attended, log_norm = attend(queries, key_rows, value_rows, allowed)
    attended_low = attended.reshape(row_count, D).astype(jnp.bfloat16)
    hidden = jnp.dot(normed, in_full, preferred_element_type=jnp.float32) + in_bias_full.astype(
        jnp.float32
    )
    active = jax.nn.gelu(hidden, approximate=True).astype(jnp.bfloat16)
    branch_attn = jnp.dot(attended_low, out_full, preferred_element_type=jnp.float32)
    branch_mlp = jnp.dot(active, fc_full, preferred_element_type=jnp.float32) + fc_bias_full.astype(
        jnp.float32
    )
    layer_out = (inputs + branch_attn + branch_mlp).astype(jnp.bfloat16)
    regathered = (
        lax.all_gather(qkv_weight, "shard", axis=0, tiled=True),
        lax.all_gather(out_weight, "shard", axis=0, tiled=True),
        lax.all_gather(in_weight, "shard", axis=0, tiled=True),
        lax.all_gather(fc_weight, "shard", axis=0, tiled=True),
        lax.all_gather(norm_gain, "shard", axis=0, tiled=True),
        lax.all_gather(norm_bias, "shard", axis=0, tiled=True),
    )
    qkv_back, out_back, in_back, fc_back, gain_back, shift_back = regathered
    upstream = cotangent * in_use[:, None].astype(jnp.bfloat16)
    grad_fc = jnp.einsum("tf,td->fd", active, upstream, preferred_element_type=jnp.float32)
    grad_fc_bias = jnp.sum(upstream.astype(jnp.float32), axis=0)
    grad_out = jnp.einsum("te,td->ed", attended_low, upstream, preferred_element_type=jnp.float32)
    grad_active = jnp.einsum("td,fd->tf", upstream, fc_back, preferred_element_type=jnp.float32)
    hidden_out, gelu_back = jax.vjp(partial(jax.nn.gelu, approximate=True), hidden)
    grad_hidden = gelu_back(grad_active)[0].astype(jnp.bfloat16)
    grad_in = jnp.einsum("td,tf->df", normed, grad_hidden, preferred_element_type=jnp.float32)
    grad_in_bias = jnp.sum(grad_hidden.astype(jnp.float32), axis=0)
    grad_attended = (
        jnp.einsum("td,ed->te", upstream, out_back, preferred_element_type=jnp.float32)
        .astype(jnp.bfloat16)
        .reshape(row_count, HEADS, HEAD_DIM)
    )
    grad_queries, grad_keys, grad_values = attend_back(
        queries, key_rows, value_rows, grad_attended, log_norm, allowed
    )
    query_back = rotate(
        grad_queries.astype(jnp.bfloat16).astype(jnp.float32), cosine, -sine_table
    ).reshape(row_count, D)
    key_back = rotate(
        grad_keys.astype(jnp.bfloat16).astype(jnp.float32), cosine, -sine_table
    ).reshape(row_count, D)
    grad_merged = jnp.concatenate(
        [query_back, key_back, grad_values.reshape(row_count, D)], -1
    ).astype(jnp.bfloat16)
    grad_qkv = jnp.einsum("td,te->de", normed, grad_merged, preferred_element_type=jnp.float32)
    grad_normed = jnp.einsum(
        "te,de->td", grad_merged, qkv_back, preferred_element_type=jnp.float32
    ) + jnp.einsum("tf,df->td", grad_hidden, in_back, preferred_element_type=jnp.float32)
    normed_again, norm_back = jax.vjp(
        layer_norm, inputs, gain_back.astype(jnp.float32), shift_back.astype(jnp.float32)
    )
    grad_inputs, grad_gain, grad_shift = norm_back(grad_normed)
    input_grad = (grad_inputs + upstream.astype(jnp.float32)).astype(jnp.bfloat16)
    rep_count = lax.axis_size("rep")
    shard_count = lax.axis_size("shard")
    grad_scale = 1.0 / math.sqrt(TOK_DEV * rep_count * shard_count)
    grad_qkv = (grad_qkv * grad_scale).astype(jnp.bfloat16)
    grad_out = (grad_out * grad_scale).astype(jnp.bfloat16)
    grad_in = (grad_in * grad_scale).astype(jnp.bfloat16)
    grad_in_bias = grad_in_bias * grad_scale
    grad_fc = (grad_fc * grad_scale).astype(jnp.bfloat16)
    grad_fc_bias = grad_fc_bias * grad_scale
    grad_gain = grad_gain * grad_scale
    grad_shift = grad_shift * grad_scale
    owner_sums = (
        lax.psum_scatter(grad_qkv, "shard", scatter_dimension=0, tiled=True),
        lax.psum_scatter(grad_out, "shard", scatter_dimension=0, tiled=True),
        lax.psum_scatter(grad_in, "shard", scatter_dimension=0, tiled=True),
        lax.psum_scatter(grad_in_bias, "shard", scatter_dimension=0, tiled=True),
        lax.psum_scatter(grad_fc, "shard", scatter_dimension=0, tiled=True),
        lax.psum_scatter(grad_fc_bias, "shard", scatter_dimension=0, tiled=True),
        lax.psum_scatter(grad_gain, "shard", scatter_dimension=0, tiled=True),
        lax.psum_scatter(grad_shift, "shard", scatter_dimension=0, tiled=True),
    )
    summed = lax.psum(
        (
            owner_sums[0],
            owner_sums[1],
            owner_sums[2],
            owner_sums[3],
            owner_sums[4],
            owner_sums[5],
            owner_sums[6],
            owner_sums[7],
        ),
        "rep",
    )
    return (
        layer_out,
        input_grad,
        summed[0].astype(jnp.float32),
        summed[1].astype(jnp.float32),
        summed[2].astype(jnp.float32),
        summed[3],
        summed[4].astype(jnp.float32),
        summed[5],
        summed[6],
        summed[7],
    )


def solution(mesh):
    in_specs = (
        P(("rep", "shard"), None),
        P(("rep", "shard")),
        P(),
        P(),
        P("shard", None),
        P("shard", None),
        P("shard", None),
        P("shard"),
        P("shard", None),
        P("shard"),
        P("shard"),
        P("shard"),
        P(("rep", "shard"), None),
    )
    out_specs = (
        P(("rep", "shard"), None),
        P(("rep", "shard"), None),
        P("shard", None),
        P("shard", None),
        P("shard", None),
        P("shard"),
        P("shard", None),
        P("shard"),
        P("shard"),
        P("shard"),
    )
    return jax.shard_map(body, mesh=mesh, in_specs=in_specs, out_specs=out_specs, check_vma=False)
```

profile of v0, /device:TPU:0, one launch (start us, length us, event | category | flops | bytes accessed | tf_op | source)
XLA Modules:
  0.0 679.0 jit_solution(2033070267634318230)
XLA Ops:
  12.2 6.0 all-gather.1
  18.2 5.4 all-gather
  25.1 9.9 %all-gather.10.cloned.1.call-done = bf16[1024,1024]{1,0:T(8,128)(2,1)} async-done(((bf16[256,1024]{1,0:T(8,128)(2,1)}), bf16[1024,1024]{1,0:T(8,128)(2,1)}) %all-gather.10.cloned.1.call-update) | async-done | bytes 2097168 | tf_op jit(solution)/shard_map/all_gather | solution.py:163
  35.0 2.9 convolution_convert_fusion
  38.4 44.5 %all-gather.8.cloned.1.call-done = bf16[1024,3072]{1,0:T(8,128)(2,1)} async-done(((bf16[256,3072]{1,0:T(8,128)(2,1)}), bf16[1024,3072]{1,0:T(8,128)(2,1)}) %all-gather.8.cloned.1.call-update) | async-done | bytes 6291472 | tf_op jit(solution)/shard_map/all_gather | solution.py:162
  82.9 5.7 fusion.98
  88.6 1.1 slice.201
  89.8 2.3 fusion.101
  92.1 3.2 copy.90
  95.3 2.4 slice.203
  97.7 2.3 slice.123
  100.0 2.9 copy.93
  102.9 2.1 slice.202
  105.0 2.3 slice.128
  107.3 1.7 copy.88
  108.9 1.8 copy.91
  110.8 1.8 copy.94
  113.8 1.6 fusion.103
  115.4 1.2 fusion.7
  116.6 1.6 fusion.102
  118.2 1.2 fusion.8
  119.4 2.3 multiply_reduce_fusion
  121.7 4.1 multiply_convert_fusion.3
  125.8 3.0 fusion.59
  128.8 2.3 multiply_reduce_fusion.1
  131.1 3.9 multiply_convert_fusion.4
  135.0 3.2 fusion.60
  138.2 1.6 copy.123
  139.8 1.5 fusion.55
  141.4 1.5 fusion.56
  144.0 2.7 multiply_convert_fusion.6
  146.7 3.7 fusion.57
  150.7 4.4 fusion.58
  158.0 1.7 slice-done.1
  159.8 1.4 fusion.52
  161.2 1.4 slice-done.3
  162.6 1.4 fusion.49
  164.2 8.8 %multiply_convert_fusion.2 = bf16[1024,3072]{1,0:T(8,128)(2,1)} fusion(bf16[512,1024]{0,1:T(8,128)(2,1)S(1)} %bitcast.90, bf16[512,1024]{0,1:T(8,128)(2,1)S(1)} %bitcast.88, bf16[512,1024]{0,1:T(8,128)(2,1)S(1)} %bitcast.86, bf16[512,1024]{1,0:T(8,128)(2,1)S(1)} %copy-done.2, f32[1024]{0:T(1024)S(1)} %bitcast.100, f32[1024]{0:T(1024)S(1)} %bitcast.93, ...), kind=kOutput, calls=%fused_computation.2 | convolution fusion | flops 3240099840 | bytes 10498048 | tf_op jit(solution)/shard_map/td,te->de/dot_general | solution.py:233
  173.6 5.8 all_gather.34
  179.4 7.2 %fusion.96 = f32[512,4096]{1,0:T(8,128)S(1)} fusion(bf16[1024,4096]{1,0:T(8,128)(2,1)} %all-gather.12.cloned.1.call-done, bf16[512,1024]{1,0:T(8,128)(2,1)S(1)} %copy-done.2, f32[1024]{0:T(1024)S(1)} %bitcast.101, f32[1024]{0:T(1024)S(1)} %bitcast.94, f32[512]{0:T(512)S(1)} %fusion.81, f32[512]{0:T(512)S(1)} %broadcast_multiply_fusion.5), kind=kOutput, calls=%fused_computation.164 | convolution fusion | flops 4298113024 | bytes 17838080 | tf_op jit(solution)/shard_map/dot_general | solution.py:189
  186.7 3.2 copy-done.35
  189.9 8.8 %multiply_convert_fusion = bf16[4096,1024]{1,0:T(8,128)(2,1)} fusion(bf16[512,1024]{1,0:T(8,128)(2,1)S(1)} %copy-done.18, bf16[512]{0:T(512)(128)(2,1)S(1)} %fusion.80, f32[512,4096]{1,0:T(8,128)S(1)} %fusion.96, f32[4096]{0:T(1024)S(1)} %convert_element_type.126), kind=kOutput, calls=%fused_computation | convolution fusion | flops 4324851712 | bytes 17843200 | tf_op jit(solution)/shard_map/tf,td->fd/dot_general | solution.py:208
  199.0 3.5 all-gather.14.cloned.1.call-done
  202.5 13.1 %convert_reduce_fusion = (f32[4096]{0:T(1024)S(1)}, bf16[512,4096]{1,0:T(8,128)(2,1)S(1)}) fusion(f32[512,4096]{1,0:T(8,128)} %copy-done.35, f32[4096]{0:T(1024)S(1)} %convert_element_type.126, bf16[4096,1024]{1,0:T(8,128)(2,1)} %all-gather.14.cloned.1.call-done, bf16[512,1024]{1,0:T(8,128)(2,1)S(1)} %copy-done.18, bf16[512]{0:T(512)(128)(2,1)S(1)} %fusion.80), kind=kOutput, calls=%fused_computation.12 | convolution fusion | flops 4343721984 | bytes 22053888 | tf_op jit(solution)/shard_map/td,fd->tf/dot_general | solution.py:211
  215.6 2.0 copy-done.36
  217.6 7.2 %multiply_convert_fusion.1 = bf16[1024,4096]{1,0:T(8,128)(2,1)} fusion(bf16[512,4096]{1,0:T(8,128)(2,1)S(1)} %get-tuple-element.57, bf16[512,1024]{1,0:T(8,128)(2,1)S(1)} %copy-done.2, f32[1024]{0:T(1024)S(1)} %bitcast.102, f32[1024]{0:T(1024)S(1)} %bitcast.95, f32[512]{0:T(512)S(1)} %fusion.81, f32[512]{0:T(512)S(1)} %broadcast_multiply_fusion.5), kind=kOutput, calls=%fused_computation.1 | convolution fusion | flops 4306501632 | bytes 13643776 | tf_op jit(solution)/shard_map/td,tf->df/dot_general | solution.py:214
  227.4 5.4 all-gather.2
  232.8 3.9 reduce-scatter.7.cloned.1.call-done
  236.7 61.3 %reduce-scatter.5.cloned.1.call-done = bf16[256,3072]{1,0:T(8,128)(2,1)} async-done(((bf16[1024,3072]{1,0:T(8,128)(2,1)}), bf16[256,3072]{1,0:T(8,128)(2,1)}) %reduce-scatter.5.cloned.1.call-update) | async-done | bytes 1572880 | tf_op jit(solution)/shard_map/reduce_scatter | solution.py:254
  297.9 74.0 %reduce-scatter.11.cloned.1.call-done = bf16[1024,1024]{1,0:T(8,128)(2,1)} async-done(((bf16[4096,1024]{1,0:T(8,128)(2,1)}), bf16[1024,1024]{1,0:T(8,128)(2,1)}) %reduce-scatter.11.cloned.1.call-update) | async-done | bytes 2097168 | tf_op jit(solution)/shard_map/reduce_scatter | solution.py:258
  371.9 74.0 %reduce-scatter.9.cloned.1.call-done = bf16[256,4096]{1,0:T(8,128)(2,1)} async-done(((bf16[1024,4096]{1,0:T(8,128)(2,1)}), bf16[256,4096]{1,0:T(8,128)(2,1)}) %reduce-scatter.9.cloned.1.call-update) | async-done | bytes 2097168 | tf_op jit(solution)/shard_map/reduce_scatter | solution.py:256
  446.0 8.4 %fusion.104 = f32[512,1024]{1,0:T(8,128)S(1)} fusion(bf16[512,4096]{1,0:T(8,128)(2,1)} %copy-done.36, bf16[1024,4096]{1,0:T(8,128)(2,1)} %all-gather.12.cloned.1.call-done), kind=kOutput, calls=%fused_computation.170 | convolution fusion | flops 4294967296 | bytes 14680064 | tf_op jit(solution)/shard_map/tf,df->td/dot_general | solution.py:236
  454.4 7.4 %fusion.100 = (f32[1024]{0:T(1024)S(1)}, f32[512]{0:T(512)S(1)}, f32[512,1024]{1,0:T(8,128)S(1)}) fusion(f32[1024]{0:T(1024)S(1)} %bitcast.96, f32[512]{0:T(512)S(1)} %broadcast_multiply_fusion.5, bf16[512,1024]{1,0:T(8,128)(2,1)S(1)} %copy-done.2, f32[512,1024]{1,0:T(8,128)S(1)} %fusion.104, bf16[1024,3072]{1,0:T(8,128)(2,1)} %all-gather.8.cloned.1.call-done, ...), kind=kOutput, calls=%fused_computation.166 | convolution fusion | flops 3234331136 | bytes 14692352 | tf_op jit(solution)/shard_map/te,de->td/dot_general | solution.py:234
  461.9 1.0 fusion.27
  462.9 1.9 convert_reduce_fusion.2
  464.9 11.1 %all-reduce.5 = (f32[4096]{0:T(1024)S(1)}, f32[1024]{0:T(1024)S(1)}, f32[1024]{0:T(1024)S(1)}, f32[1024]{0:T(1024)S(1)}) all-reduce(f32[4096]{0:T(1024)S(1)} %broadcast_multiply_fusion.1, f32[1024]{0:T(1024)S(1)} %broadcast_multiply_fusion.4, ...), channel_id=5, replica_groups=mesh['rep'=8,'shard'=4] {'shard'}, use_global_device_ids=true, to_apply=%region_20.21.clone | all-reduce | flops 7168 | bytes 57344
  476.2 23.9 %all-reduce.4 = (f32[1024]{0:T(1024)}, f32[256]{0:T(256)}, f32[256]{0:T(256)}, f32[256]{0:T(256)}) all-reduce(f32[1024]{0:T(1024)S(1)} %dynamic-slice.1, f32[256]{0:T(256)S(1)} %dynamic-slice.3, f32[256]{0:T(256)S(1)} %dynamic-slice.5, f32[256]{0:T(256)S(1)} %dynamic-slice.7), channel_id=1, replica_groups=mesh['rep'=8,'shard'=4] {'rep'}, use_global_device_ids=true, to_apply=%region_21.22 | all-reduce | flops 1792 | bytes 14336 | tf_op jit(solution)/shard_map/psum | solution.py:263
  500.1 10.6 %fusion.93 = f32[512,1024]{1,0:T(8,128)S(1)} fusion(bf16[4096,1024]{1,0:T(8,128)(2,1)} %all-gather.14.cloned.1.call-done, f32[512,4096]{1,0:T(8,128)} %copy-done.35, f32[4096]{0:T(1024)S(1)} %convert_element_type.126), kind=kOutput, calls=%fused_computation.163 | convolution fusion | flops 4315938816 | bytes 18890752 | tf_op jit(solution)/shard_map/dot_general | solution.py:194
  510.7 2.4 fusion.32
  513.1 148.4 %all-reduce.9.cloned.1.call-done = (bf16[256,3072]{1,0:T(8,128)(2,1)}, bf16[256,1024]{1,0:T(8,128)(2,1)}, bf16[256,4096]{1,0:T(8,128)(2,1)}, bf16[1024,1024]{1,0:T(8,128)(2,1)}) async-done(((bf16[256,3072]{1,0:T(8,128)(2,1)}, bf16[256,1024]{1,0:T(8,128)(2,1)}, bf16[256,4096]{1,0:T(8,128)(2,1)}, bf16[1024,1024]{1,0:T(8,128)(2,1)}), (bf16[256,3072]{1,0:T(8,128)(2,1)}, bf16[256,1024]{1,0:T(8,128)(2,1)}, ...) | async-done | bytes 6291472 | tf_op jit(solution)/shard_map/psum | solution.py:263
  661.6 2.3 convert_element_type.142
  663.8 3.4 convert_element_type.140
  667.3 2.5 convert_element_type.144
  669.8 2.5 convert_element_type.147
  (152 shorter events, 14.8 us)
Async XLA Ops:
  7.2 2.9 copy-start.29
  7.2 3.0 copy-start.28
  7.2 4.2 copy-start.31
  7.2 4.3 copy-start.32
  7.2 4.3 copy-start.27
  7.2 4.3 copy-start.2
  7.2 27.7 %all-gather.10.cloned.1.call-start = ((), (), s32[]{:S(2)}) async-start(), calls=%async_computation.5 | async-start | bytes 2621440 | tf_op jit(solution)/shard_map/all_gather | solution.py:163
  8.0 27.0 %copy-start.16 = (bf16[512,1024]{1,0:T(8,128)(2,1)S(1)}, bf16[512,1024]{1,0:T(8,128)(2,1)}, u32[]{:S(2)}) copy-start(bf16[512,1024]{1,0:T(8,128)(2,1)} %param.25) | copy-start | bytes 3145732
  8.0 74.9 %all-gather.8.cloned.1.call-start = ((), (), s32[]{:S(2)}) async-start(), calls=%async_computation.4 | async-start | bytes 7864320 | tf_op jit(solution)/shard_map/all_gather | solution.py:162
  8.7 170.7 %all-gather.12.cloned.1.call-start = ((), (), s32[]{:S(2)}) async-start(), calls=%async_computation.6 | async-start | bytes 10485760 | tf_op jit(solution)/shard_map/all_gather | solution.py:164
  9.5 193.0 %all-gather.14.cloned.1.call-start = ((), (), s32[]{:S(2)}) async-start(), calls=%async_computation.7 | async-start | bytes 10485760 | tf_op jit(solution)/shard_map/all_gather | solution.py:166
  10.0 226.6 %reduce-scatter.7.cloned.1.call-start = ((), (), s32[]{:S(2)}) async-start(), calls=%async_computation.9 | async-start | bytes 2621440 | tf_op jit(solution)/shard_map/reduce_scatter | solution.py:255
  12.1 11.4 %copy-start.24 = (f32[512]{0:T(512)}, f32[512]{0:T(512)S(1)}, u32[]{:S(2)}) copy-start(f32[512]{0:T(512)S(1)} %fusion.29) | copy-start | bytes 6148
  112.6 1.1 copy-start.19
  112.6 1.2 copy-start.22
  113.4 3.2 copy-start.21
  113.8 12.0 %copy-start.23 = (bf16[512,16,32]{0,2,1:T(8,128)(2,1)}, bf16[512,16,32]{0,2,1:T(8,128)(2,1)S(1)}, u32[]{:S(2)}) copy-start(bf16[512,16,32]{0,2,1:T(8,128)(2,1)S(1)} %copy.120) | copy-start | bytes 1572868
  115.4 24.4 %copy-start = (f32[8,512,512]{1,2,0:T(8,128)}, f32[8,512,512]{1,2,0:T(8,128)S(1)}, u32[]{:S(2)}) copy-start(f32[8,512,512]{1,2,0:T(8,128)S(1)} %get-tuple-element.50) | copy-start | bytes 25165828
  118.2 23.1 %copy-start.1 = (f32[8,512,512]{1,2,0:T(8,128)}, f32[8,512,512]{1,2,0:T(8,128)S(1)}, u32[]{:S(2)}) copy-start(f32[8,512,512]{1,2,0:T(8,128)S(1)} %get-tuple-element.48) | copy-start | bytes 25165828
  128.8 9.3 %copy-start.6 = (bf16[512,8,64]{0,2,1:T(8,128)(2,1)}, bf16[512,8,64]{0,2,1:T(8,128)(2,1)S(1)}, u32[]{:S(2)}) copy-start(bf16[512,8,64]{0,2,1:T(8,128)(2,1)S(1)} %fusion.59) | copy-start | bytes 1572868
  138.1 3.2 copy-start.8
  141.4 2.6 copy-start.17
  143.0 1.0 copy-start.10
  144.0 2.7 copy-start.20
  150.3 147.6 %reduce-scatter.5.cloned.1.call-start = ((), (), s32[]{:S(2)}) async-start(), calls=%async_computation.8 | async-start | bytes 7864320 | tf_op jit(solution)/shard_map/reduce_scatter | solution.py:254
  150.6 5.2 copy-start.3
  155.1 2.9 slice-start
  155.8 1.7 copy-start.7
  155.8 1.9 copy-start.9
  156.2 3.6 slice-start.1
  157.8 6.3 copy-start.12
  157.8 3.4 slice-start.2
  159.8 4.4 copy-start.14
  159.8 2.9 slice-start.3
  172.9 0.7 copy-start.26
  173.0 199.0 %reduce-scatter.11.cloned.1.call-start = ((), (), s32[]{:S(2)}) async-start(), calls=%async_computation.11 | async-start | bytes 10485760 | tf_op jit(solution)/shard_map/reduce_scatter | solution.py:258
  179.4 10.5 %copy-start.18 = (bf16[512,1024]{1,0:T(8,128)(2,1)S(1)}, bf16[512,1024]{1,0:T(8,128)(2,1)}, u32[]{:S(2)}) copy-start(bf16[512,1024]{1,0:T(8,128)(2,1)} %param.25) | copy-start | bytes 3145732
  186.7 3.2 copy-start.35
  198.8 247.2 %reduce-scatter.9.cloned.1.call-start = ((), (), s32[]{:S(2)}) async-start(), calls=%async_computation.10 | async-start | bytes 10485760 | tf_op jit(solution)/shard_map/reduce_scatter | solution.py:256
  215.6 2.0 copy-start.36
  224.8 0.7 copy-start.34
  224.8 2.5 copy-start.33
  224.9 436.7 %all-reduce.9.cloned.1.call-start = ((), (), s32[]{:S(2)}) async-start(), calls=%async_computation.12 | async-start | bytes 12582912 | tf_op jit(solution)/shard_map/psum | solution.py:263
  446.0 8.4 %copy-start.13 = (bf16[512,16,64]{0,2,1:T(8,128)(2,1)S(1)}, bf16[512,16,64]{0,2,1:T(8,128)(2,1)}, u32[]{:S(2)}) copy-start(bf16[512,16,64]{0,2,1:T(8,128)(2,1)} %copy-done.12) | copy-start | bytes 3145732
  446.0 8.4 %copy-start.15 = (bf16[512,16,64]{0,2,1:T(8,128)(2,1)S(1)}, bf16[512,16,64]{0,2,1:T(8,128)(2,1)}, u32[]{:S(2)}) copy-start(bf16[512,16,64]{0,2,1:T(8,128)(2,1)} %copy-done.14) | copy-start | bytes 3145732
  454.4 7.5 %copy-start.25 = (f32[512]{0:T(512)S(1)}, f32[512]{0:T(512)}, u32[]{:S(2)}) copy-start(f32[512]{0:T(512)} %copy-done.24) | copy-start | bytes 6148
  500.1 10.6 %copy-start.11 = (bf16[512,16,64]{0,2,1:T(8,128)(2,1)S(1)}, bf16[512,16,64]{0,2,1:T(8,128)(2,1)}, u32[]{:S(2)}) copy-start(bf16[512,16,64]{0,2,1:T(8,128)(2,1)} %copy-done.10) | copy-start | bytes 3145732
  500.1 10.7 %copy-start.30 = (bf16[1024,1024]{1,0:T(8,128)(2,1)S(1)}, bf16[1024,1024]{1,0:T(8,128)(2,1)}, u32[]{:S(2)}) copy-start(bf16[1024,1024]{1,0:T(8,128)(2,1)} %all-gather.10.cloned.1.call-done) | copy-start | bytes 6291460
  661.5 5.7 copy-start.5
  667.3 2.5 copy-start.4
Sparse Core Ops, SparseCore 0:
  9.6 25.2 all-gather.9
  36.5 46.3 all-gather.7
  84.5 58.2 all-gather.11
  144.2 58.2 all-gather.13
  205.5 31.1 reduce-scatter.6
  239.1 58.8 reduce-scatter.4
  300.5 71.3 reduce-scatter.10
  374.5 71.3 reduce-scatter.8
  450.4 211.0 all-reduce.8
where the time goes:
time: 685 us; the launch traced here: 679 us
  waiting for transfers between devices  422 us (62%)
  matrix products  113 us (16%)
  blocking collectives  57.6 us (8%)
  local copies, waits for them, and re-layouts  40.4 us (6%)
  other arithmetic  28.8 us (4%)
  between operations  16.2 us (2%)
    psum x1, waiting for transfers between devices, body(): lax.psum((owner_sums[0], owner_sums[1], owner_sums[2], owner_sums[3], own...  148 us
    reduce_scatter x1, waiting for transfers between devices, body(): lax.psum_scatter(grad_fc, 'shard', scatter_dimension=0, tiled=True)  74 us
    reduce_scatter x1, waiting for transfers between devices, body(): lax.psum_scatter(grad_in, 'shard', scatter_dimension=0, tiled=True)  74 us
    reduce_scatter x1, waiting for transfers between devices, body(): lax.psum_scatter(grad_qkv, 'shard', scatter_dimension=0, tiled=True)  61.3 us
    all_gather x1, waiting for transfers between devices, body(): lax.all_gather(qkv_weight, 'shard', axis=0, tiled=True)  44.5 us
    psum x1, blocking collectives, body(): lax.psum((owner_sums[0], owner_sums[1], owner_sums[2], owner_sums[3], own...  23.9 us
  transfers between devices with their start and end apart: 9, of which 8 were waited for; matrix products, arithmetic and copies ran while one was open for 24% of the time, Pallas kernels for 0%

commit v1 on v0

--- a/solution.py
+++ b/solution.py
@@ -13,6 +13,24 @@
 EPS = 1e-05
 NEG = -1000000000.0
 SCORE_SCALE = 0.125
+
+
+def collect(shard, axis, dim):
+    ways, here, turn = (lax.axis_size(axis), lax.axis_index(axis), shard.shape[dim])
+    lengths = [n * ways if d == dim else n for d, n in enumerate(shard.shape)]
+    full = lax.dynamic_update_slice_in_dim(
+        jnp.zeros(lengths, shard.dtype), shard, here * turn, axis=dim
+    )
+    going_up = going_down = shard
+    for far in range(1, ways // 2 + 1):
+        going_up = lax.ppermute(going_up, axis, [(d, (d + 1) % ways) for d in range(ways)])
+        full = lax.dynamic_update_slice_in_dim(full, going_up, (here - far) % ways * turn, axis=dim)
+        if 2 * far < ways:
+            going_down = lax.ppermute(going_down, axis, [(d, (d - 1) % ways) for d in range(ways)])
+            full = lax.dynamic_update_slice_in_dim(
+                full, going_down, (here + far) % ways * turn, axis=dim
+            )
+    return full
 
 
 def layout(lengths, owner, device):
@@ -159,7 +177,7 @@
     slot_index = jnp.arange(row_count, dtype=jnp.int32)
     allowed = (segment[:, None] == segment[None, :]) & (slot_index[None, :] <= slot_index[:, None])
     gathered = (
-        lax.all_gather(qkv_weight, "shard", axis=0, tiled=True),
+        collect(qkv_weight, "shard", 0),
         lax.all_gather(out_weight, "shard", axis=0, tiled=True),
         lax.all_gather(in_weight, "shard", axis=0, tiled=True),
         lax.all_gather(in_bias, "shard", axis=0, tiled=True),

time: 685 us -> 717 us (1.047)
  blocking collectives: 57.6 us -> 97.8 us
  waiting for transfers between devices: 422 us -> 406 us
    ppermute x0 -> x3, waiting for transfers between devices: none -> 48.5 us  [the longest x2 48.5 us: collect(): lax.ppermute(going_up, axis, [(d, (d + 1) % ways) for d in range(ways)])]
    reduce_scatter x1, waiting for transfers between devices: 61.3 us -> 14.7 us  [body(): lax.psum_scatter(grad_qkv, 'shard', scatter_dimension=0, tiled=True)]
    all_gather x1, blocking collectives: 6.04 us -> 45 us  [body(): lax.all_gather(norm_bias, 'shard', axis=0, tiled=True)]
    all_gather x1, waiting for transfers between devices: 9.87 us -> 0.01 us  [body(): lax.all_gather(out_weight, 'shard', axis=0, tiled=True)]
    psum x1, waiting for transfers between devices: 148 us -> 156 us  [body(): lax.psum((owner_sums[0], owner_sums[1], owner_sums[2], owner_sums[3], own...]
    all_gather x1, waiting for transfers between devices: 44.5 us -> 37.3 us  [body(): lax.all_gather(qkv_weight, 'shard', axis=0, tiled=True)]
  transfers between devices with their start and end apart: 9 -> 12, of which waited for: 8 -> 6; matrix products, arithmetic and copies ran while one was open for 24% -> 23% of each run, Pallas kernels for 0% -> 0%
where the time goes in v1:
time: 717 us; the launch traced here: 710 us
  waiting for transfers between devices  406 us (57%)
  matrix products  113 us (16%)
  blocking collectives  97.8 us (14%)
  local copies, waits for them, and re-layouts  43.6 us (6%)
  other arithmetic  29 us (4%)
  between operations  16.2 us (2%)
    psum x1, waiting for transfers between devices, body(): lax.psum((owner_sums[0], owner_sums[1], owner_sums[2], owner_sums[3], own...  156 us
    reduce_scatter x1, waiting for transfers between devices, body(): lax.psum_scatter(grad_in, 'shard', scatter_dimension=0, tiled=True)  74 us
    reduce_scatter x1, waiting for transfers between devices, body(): lax.psum_scatter(grad_fc, 'shard', scatter_dimension=0, tiled=True)  73.9 us
    ppermute x2, waiting for transfers between devices, collect(): lax.ppermute(going_up, axis, [(d, (d + 1) % ways) for d in range(ways)])  48.5 us
    all_gather x1, blocking collectives, body(): lax.all_gather(norm_bias, 'shard', axis=0, tiled=True)  45 us
    all_gather x1, waiting for transfers between devices, body(): lax.all_gather(qkv_weight, 'shard', axis=0, tiled=True)  37.3 us
    psum x1, blocking collectives, body(): lax.psum((owner_sums[0], owner_sums[1], owner_sums[2], owner_sums[3], own...  24.4 us
    reduce_scatter x1, waiting for transfers between devices, body(): lax.psum_scatter(grad_qkv, 'shard', scatter_dimension=0, tiled=True)  14.7 us
  transfers between devices with their start and end apart: 12, of which 6 were waited for; matrix products, arithmetic and copies ran while one was open for 23% of the time, Pallas kernels for 0%

profile of v1, /device:TPU:0, one launch (start us, length us, event | category | flops | bytes accessed | tf_op | source)
XLA Modules:
  0.0 710.0 jit_solution(5817289155114892098)
XLA Ops:
  9.3 2.0 collective-permute-start.1
  13.5 45.0 %all-gather.1 = bf16[4,1,256]{2,1,0:T(2,128)(2,1)S(1)} all-gather(bf16[1,1,256]{2,1,0:T(2,128)(2,1)S(1)} %reshape.318), channel_id=1, replica_groups=mesh['rep'=8,'shard'=4] {'shard'}, dimensions={0}, use_global_device_ids=true | all-gather | bytes 2560 | tf_op jit(solution)/shard_map/all_gather | solution.py:187
  58.5 6.1 all-gather
  67.5 1.6 constant_dynamic-update-slice_fusion.2
  69.1 1.6 constant_dynamic-update-slice_fusion.1
  70.7 48.5 %collective-permute-done.2 = bf16[256,3072]{1,0:T(8,128)(2,1)S(1)} collective-permute-done((bf16[256,3072]{1,0:T(8,128)(2,1)}, bf16[256,3072]{1,0:T(8,128)(2,1)S(1)}, u32[]{:S(2)}, u32[]{:S(2)}) %collective-permute-start.2) | collective-permute-done | bytes 1572896 | tf_op jit(solution)/shard_map/ppermute | solution.py:26
  119.4 3.6 fusion.98
  123.0 1.1 slice.201
  124.1 1.8 fusion.101
  125.9 2.9 copy.90
  128.8 2.1 slice.203
  130.8 2.4 slice.123
  133.3 1.8 copy.93
  135.1 2.4 slice.202
  137.5 2.3 slice.128
  139.8 3.2 convolution_convert_fusion
  143.6 1.8 copy.88
  145.4 1.8 copy.91
  147.2 1.8 copy.94
  150.2 1.6 fusion.103
  151.8 1.2 fusion.7
  153.1 1.6 fusion.102
  154.6 1.2 fusion.8
  155.9 2.3 multiply_reduce_fusion
  158.1 4.3 multiply_convert_fusion.3
  162.5 3.0 fusion.59
  165.5 2.3 multiply_reduce_fusion.1
  167.8 3.9 multiply_convert_fusion.4
  171.6 3.1 fusion.60
  174.8 1.6 copy.123
  176.4 1.5 fusion.55
  178.0 1.5 fusion.56
  180.6 2.7 multiply_convert_fusion.6
  183.2 3.7 fusion.57
  187.2 3.7 fusion.58
  193.4 2.0 slice-done.1
  195.4 1.4 fusion.52
  197.1 1.5 slice-done.3
  198.6 1.4 fusion.49
  201.1 8.7 %multiply_convert_fusion.2 = bf16[1024,3072]{1,0:T(8,128)(2,1)} fusion(bf16[512,1024]{0,1:T(8,128)(2,1)S(1)} %bitcast.90, bf16[512,1024]{0,1:T(8,128)(2,1)S(1)} %bitcast.88, bf16[512,1024]{0,1:T(8,128)(2,1)S(1)} %bitcast.86, bf16[512,1024]{1,0:T(8,128)(2,1)S(1)} %copy-done.2, f32[1024]{0:T(1024)S(1)} %bitcast.100, f32[1024]{0:T(1024)S(1)} %bitcast.93, ...), kind=kOutput, calls=%fused_computation.2 | convolution fusion | flops 3240099840 | bytes 10498048 | tf_op jit(solution)/shard_map/td,te->de/dot_general | solution.py:251
  210.5 5.6 all_gather.32
  216.1 7.3 %fusion.96 = f32[512,4096]{1,0:T(8,128)S(1)} fusion(bf16[1024,4096]{1,0:T(8,128)(2,1)} %all-gather.10.cloned.1.call-done, bf16[512,1024]{1,0:T(8,128)(2,1)S(1)} %copy-done.2, f32[1024]{0:T(1024)S(1)} %bitcast.101, f32[1024]{0:T(1024)S(1)} %bitcast.94, f32[512]{0:T(512)S(1)} %fusion.81, f32[512]{0:T(512)S(1)} %broadcast_multiply_fusion.5), kind=kOutput, calls=%fused_computation.168 | convolution fusion | flops 4298113024 | bytes 17838080 | tf_op jit(solution)/shard_map/dot_general | solution.py:207
  223.4 3.2 copy-done.37
  226.6 8.8 %multiply_convert_fusion = bf16[4096,1024]{1,0:T(8,128)(2,1)} fusion(bf16[512,1024]{1,0:T(8,128)(2,1)S(1)} %copy-done.19, bf16[512]{0:T(512)(128)(2,1)S(1)} %fusion.80, f32[512,4096]{1,0:T(8,128)S(1)} %fusion.96, f32[4096]{0:T(1024)S(1)} %convert_element_type.126), kind=kOutput, calls=%fused_computation | convolution fusion | flops 4324851712 | bytes 17843200 | tf_op jit(solution)/shard_map/tf,td->fd/dot_general | solution.py:226
  235.8 13.1 %convert_reduce_fusion = (f32[4096]{0:T(1024)S(1)}, bf16[512,4096]{1,0:T(8,128)(2,1)S(1)}) fusion(f32[512,4096]{1,0:T(8,128)} %copy-done.37, f32[4096]{0:T(1024)S(1)} %convert_element_type.126, bf16[4096,1024]{1,0:T(8,128)(2,1)} %all-gather.12.cloned.1.call-done, bf16[512,1024]{1,0:T(8,128)(2,1)S(1)} %copy-done.19, bf16[512]{0:T(512)(128)(2,1)S(1)} %fusion.80), kind=kOutput, calls=%fused_computation.12 | convolution fusion | flops 4343721984 | bytes 22053888 | tf_op jit(solution)/shard_map/td,fd->tf/dot_general | solution.py:229
  248.9 2.0 copy-done.38
  250.9 7.3 %multiply_convert_fusion.1 = bf16[1024,4096]{1,0:T(8,128)(2,1)} fusion(bf16[512,4096]{1,0:T(8,128)(2,1)S(1)} %get-tuple-element.57, bf16[512,1024]{1,0:T(8,128)(2,1)S(1)} %copy-done.2, f32[1024]{0:T(1024)S(1)} %bitcast.102, f32[1024]{0:T(1024)S(1)} %bitcast.95, f32[512]{0:T(512)S(1)} %fusion.81, f32[512]{0:T(512)S(1)} %broadcast_multiply_fusion.5), kind=kOutput, calls=%fused_computation.1 | convolution fusion | flops 4306501632 | bytes 13643776 | tf_op jit(solution)/shard_map/td,tf->df/dot_general | solution.py:232
  261.0 5.5 all-gather.2
  266.5 14.7 %reduce-scatter.5.cloned.1.call-done = bf16[256,3072]{1,0:T(8,128)(2,1)} async-done(((bf16[1024,3072]{1,0:T(8,128)(2,1)}), bf16[256,3072]{1,0:T(8,128)(2,1)}) %reduce-scatter.5.cloned.1.call-update) | async-done | bytes 1572880 | tf_op jit(solution)/shard_map/reduce_scatter | solution.py:272
  281.2 73.9 %reduce-scatter.11.cloned.1.call-done = bf16[1024,1024]{1,0:T(8,128)(2,1)} async-done(((bf16[4096,1024]{1,0:T(8,128)(2,1)}), bf16[1024,1024]{1,0:T(8,128)(2,1)}) %reduce-scatter.11.cloned.1.call-update) | async-done | bytes 2097168 | tf_op jit(solution)/shard_map/reduce_scatter | solution.py:276
  355.1 74.0 %reduce-scatter.9.cloned.1.call-done = bf16[256,4096]{1,0:T(8,128)(2,1)} async-done(((bf16[1024,4096]{1,0:T(8,128)(2,1)}), bf16[256,4096]{1,0:T(8,128)(2,1)}) %reduce-scatter.9.cloned.1.call-update) | async-done | bytes 2097168 | tf_op jit(solution)/shard_map/reduce_scatter | solution.py:274
  429.1 10.6 %fusion.104 = f32[512,1024]{1,0:T(8,128)} fusion(bf16[512,4096]{1,0:T(8,128)(2,1)} %copy-done.38, bf16[1024,4096]{1,0:T(8,128)(2,1)} %all-gather.10.cloned.1.call-done), kind=kOutput, calls=%fused_computation.174 | convolution fusion | flops 4294967296 | bytes 14680064 | tf_op jit(solution)/shard_map/tf,df->td/dot_general | solution.py:254
  439.8 37.3 %all-gather.14.cloned.1.call-done = bf16[1024,3072]{1,0:T(8,128)(2,1)} async-done(((bf16[256,3072]{1,0:T(8,128)(2,1)}), bf16[1024,3072]{1,0:T(8,128)(2,1)}) %all-gather.14.cloned.1.call-update) | async-done | bytes 6291472 | tf_op jit(solution)/shard_map/all_gather | solution.py:217
  477.0 7.6 %fusion.100 = (f32[1024]{0:T(1024)S(1)}, f32[512]{0:T(512)S(1)}, f32[512,1024]{1,0:T(8,128)S(1)}) fusion(f32[1024]{0:T(1024)S(1)} %bitcast.96, f32[512]{0:T(512)S(1)} %broadcast_multiply_fusion.5, bf16[512,1024]{1,0:T(8,128)(2,1)S(1)} %copy-done.2, f32[512,1024]{1,0:T(8,128)} %fusion.104, bf16[1024,3072]{1,0:T(8,128)(2,1)} %all-gather.14.cloned.1.call-done, ...), kind=kOutput, calls=%fused_computation.170 | convolution fusion | flops 3234331136 | bytes 14692352 | tf_op jit(solution)/shard_map/te,de->td/dot_general | solution.py:252
  485.7 1.9 convert_reduce_fusion.2
  487.7 11.2 %all-reduce.5 = (f32[4096]{0:T(1024)S(1)}, f32[1024]{0:T(1024)S(1)}, f32[1024]{0:T(1024)S(1)}, f32[1024]{0:T(1024)S(1)}) all-reduce(f32[4096]{0:T(1024)S(1)} %broadcast_multiply_fusion.1, f32[1024]{0:T(1024)S(1)} %broadcast_multiply_fusion.4, ...), channel_id=5, replica_groups=mesh['rep'=8,'shard'=4] {'shard'}, use_global_device_ids=true, to_apply=%region_20.21.clone | all-reduce | flops 7168 | bytes 57344
  499.1 24.4 %all-reduce.4 = (f32[1024]{0:T(1024)}, f32[256]{0:T(256)}, f32[256]{0:T(256)}, f32[256]{0:T(256)}) all-reduce(f32[1024]{0:T(1024)S(1)} %dynamic-slice.1, f32[256]{0:T(256)S(1)} %dynamic-slice.3, f32[256]{0:T(256)S(1)} %dynamic-slice.5, f32[256]{0:T(256)S(1)} %dynamic-slice.7), channel_id=1, replica_groups=mesh['rep'=8,'shard'=4] {'rep'}, use_global_device_ids=true, to_apply=%region_21.22 | all-reduce | flops 1792 | bytes 14336 | tf_op jit(solution)/shard_map/psum | solution.py:281
  523.5 10.8 %fusion.93 = f32[512,1024]{1,0:T(8,128)S(1)} fusion(bf16[4096,1024]{1,0:T(8,128)(2,1)} %all-gather.12.cloned.1.call-done, f32[512,4096]{1,0:T(8,128)} %copy-done.37, f32[4096]{0:T(1024)S(1)} %convert_element_type.126), kind=kOutput, calls=%fused_computation.167 | convolution fusion | flops 4315938816 | bytes 18890752 | tf_op jit(solution)/shard_map/dot_general | solution.py:212
  534.4 2.4 fusion.32
  536.7 155.9 %all-reduce.9.cloned.1.call-done = (bf16[256,3072]{1,0:T(8,128)(2,1)}, bf16[256,1024]{1,0:T(8,128)(2,1)}, bf16[256,4096]{1,0:T(8,128)(2,1)}, bf16[1024,1024]{1,0:T(8,128)(2,1)}) async-done(((bf16[256,3072]{1,0:T(8,128)(2,1)}, bf16[256,1024]{1,0:T(8,128)(2,1)}, bf16[256,4096]{1,0:T(8,128)(2,1)}, bf16[1024,1024]{1,0:T(8,128)(2,1)}), (bf16[256,3072]{1,0:T(8,128)(2,1)}, bf16[256,1024]{1,0:T(8,128)(2,1)}, ...) | async-done | bytes 6291472 | tf_op jit(solution)/shard_map/psum | solution.py:281
  692.6 2.3 convert_element_type.142
  694.9 3.4 convert_element_type.140
  698.3 2.5 convert_element_type.144
  700.8 2.5 convert_element_type.147
  (167 shorter events, 17.6 us)
Async XLA Ops:
  7.2 4.2 copy-start.31
  7.2 4.2 copy-start.30
  7.2 5.5 copy-start.2
  7.2 6.3 copy-start.33
  7.2 6.3 copy-start.34
  7.2 6.3 copy-start.29
  7.2 132.6 %all-gather.8.cloned.1.call-start = ((), (), s32[]{:S(2)}) async-start(), calls=%async_computation.4 | async-start | bytes 2621440 | tf_op jit(solution)/shard_map/all_gather | solution.py:181
  8.0 208.1 %all-gather.10.cloned.1.call-start = ((), (), s32[]{:S(2)}) async-start(), calls=%async_computation.5 | async-start | bytes 10485760 | tf_op jit(solution)/shard_map/all_gather | solution.py:182
  8.7 227.1 %all-gather.12.cloned.1.call-start = ((), (), s32[]{:S(2)}) async-start(), calls=%async_computation.6 | async-start | bytes 10485760 | tf_op jit(solution)/shard_map/all_gather | solution.py:184
  8.8 56.5 %collective-permute-start = (bf16[256,3072]{1,0:T(8,128)(2,1)}, bf16[256,3072]{1,0:T(8,128)(2,1)}, u32[]{:S(2)}, u32[]{:S(2)}) collective-permute-start(bf16[256,3072]{1,0:T(8,128)(2,1)} %param.17), channel_id=1, source_target_pairs={{0,1},{1,2},{2,3},{3,0},{4,5},{5,6},{6,7},{7,4},{8,9},{9,10},{10,1... | collective-permute-start | bytes 4718600 | tf_op jit(solution)/shard_map/ppermute | solution.py:26
  9.3 59.8 %collective-permute-start.1 = (bf16[256,3072]{1,0:T(8,128)(2,1)}, bf16[256,3072]{1,0:T(8,128)(2,1)}, u32[]{:S(2)}, u32[]{:S(2)}) collective-permute-start(bf16[256,3072]{1,0:T(8,128)(2,1)} %param.17), channel_id=1, source_target_pairs={{0,3},{1,0},{2,1},{3,2},{4,7},{5,4},{6,5},{7,6},{8,11},{9,8},{10,9... | collective-permute-start | bytes 4718600 | tf_op jit(solution)/shard_map/ppermute | solution.py:29
  11.3 255.2 %reduce-scatter.7.cloned.1.call-start = ((), (), s32[]{:S(2)}) async-start(), calls=%async_computation.9 | async-start | bytes 2621440 | tf_op jit(solution)/shard_map/reduce_scatter | solution.py:273
  12.9 54.4 %copy-start.3 = (bf16[256,3072]{1,0:T(8,128)(2,1)S(1)}, bf16[256,3072]{1,0:T(8,128)(2,1)}, u32[]{:S(2)}) copy-start(bf16[256,3072]{1,0:T(8,128)(2,1)} %param.17) | copy-start | bytes 4718596
  13.4 51.3 %copy-start.26 = (f32[512]{0:T(512)}, f32[512]{0:T(512)S(1)}, u32[]{:S(2)}) copy-start(f32[512]{0:T(512)S(1)} %fusion.29) | copy-start | bytes 6148
  65.3 53.9 %collective-permute-start.2 = (bf16[256,3072]{1,0:T(8,128)(2,1)}, bf16[256,3072]{1,0:T(8,128)(2,1)S(1)}, u32[]{:S(2)}, u32[]{:S(2)}) collective-permute-start(bf16[256,3072]{1,0:T(8,128)(2,1)} %collective-permute-done), channel_id=1, source_target_pairs={{0,1},{1,2},{2,3},{3,0},{4,5},{5,6},{6,7},{7,4},{8,9},{9,10},{10,1... | collective-permute-start | bytes 4718600 | tf_op jit(solution)/shard_map/ppermute | solution.py:26
  149.0 1.1 copy-start.21
  149.0 1.2 copy-start.23
  149.9 3.2 copy-start.24
  150.2 12.2 %copy-start.25 = (bf16[512,16,32]{0,2,1:T(8,128)(2,1)}, bf16[512,16,32]{0,2,1:T(8,128)(2,1)S(1)}, u32[]{:S(2)}) copy-start(bf16[512,16,32]{0,2,1:T(8,128)(2,1)S(1)} %copy.120) | copy-start | bytes 1572868
  151.8 24.6 %copy-start = (f32[8,512,512]{1,2,0:T(8,128)}, f32[8,512,512]{1,2,0:T(8,128)S(1)}, u32[]{:S(2)}) copy-start(f32[8,512,512]{1,2,0:T(8,128)S(1)} %get-tuple-element.50) | copy-start | bytes 25165828
  154.6 23.3 %copy-start.1 = (f32[8,512,512]{1,2,0:T(8,128)}, f32[8,512,512]{1,2,0:T(8,128)S(1)}, u32[]{:S(2)}) copy-start(f32[8,512,512]{1,2,0:T(8,128)S(1)} %get-tuple-element.48) | copy-start | bytes 25165828
  165.5 9.3 %copy-start.7 = (bf16[512,8,64]{0,2,1:T(8,128)(2,1)}, bf16[512,8,64]{0,2,1:T(8,128)(2,1)S(1)}, u32[]{:S(2)}) copy-start(bf16[512,8,64]{0,2,1:T(8,128)(2,1)S(1)} %fusion.59) | copy-start | bytes 1572868
  174.7 3.2 copy-start.9
  178.0 2.6 copy-start.18
  179.6 1.0 copy-start.11
  180.6 2.7 copy-start.22
  186.9 94.3 %reduce-scatter.5.cloned.1.call-start = ((), (), s32[]{:S(2)}) async-start(), calls=%async_computation.8 | async-start | bytes 7864320 | tf_op jit(solution)/shard_map/reduce_scatter | solution.py:272
  187.2 4.5 copy-start.4
  190.9 2.5 slice-start
  191.6 1.4 copy-start.8
  191.6 1.5 copy-start.10
  192.0 3.4 slice-start.1
  193.2 6.9 copy-start.13
  193.3 3.8 slice-start.2
  195.4 4.8 copy-start.15
  195.4 3.2 slice-start.3
  200.2 1.0 copy-start.17
  209.8 0.7 copy-start.28
  209.9 145.2 %reduce-scatter.11.cloned.1.call-start = ((), (), s32[]{:S(2)}) async-start(), calls=%async_computation.11 | async-start | bytes 10485760 | tf_op jit(solution)/shard_map/reduce_scatter | solution.py:276
  216.1 10.5 %copy-start.19 = (bf16[512,1024]{1,0:T(8,128)(2,1)S(1)}, bf16[512,1024]{1,0:T(8,128)(2,1)}, u32[]{:S(2)}) copy-start(bf16[512,1024]{1,0:T(8,128)(2,1)} %param.25) | copy-start | bytes 3145732
  223.4 3.2 copy-start.37
  235.5 193.6 %reduce-scatter.9.cloned.1.call-start = ((), (), s32[]{:S(2)}) async-start(), calls=%async_computation.10 | async-start | bytes 10485760 | tf_op jit(solution)/shard_map/reduce_scatter | solution.py:274
  248.9 2.0 copy-start.38
  258.2 0.8 copy-start.36
  258.2 2.7 copy-start.35
  258.3 218.8 %all-gather.14.cloned.1.call-start = ((), (), s32[]{:S(2)}) async-start(), calls=%async_computation.7 | async-start | bytes 7864320 | tf_op jit(solution)/shard_map/all_gather | solution.py:217
  259.0 433.6 %all-reduce.9.cloned.1.call-start = ((), (), s32[]{:S(2)}) async-start(), calls=%async_computation.12 | async-start | bytes 12582912 | tf_op jit(solution)/shard_map/psum | solution.py:281
  429.1 47.9 %copy-start.14 = (bf16[512,16,64]{0,2,1:T(8,128)(2,1)S(1)}, bf16[512,16,64]{0,2,1:T(8,128)(2,1)}, u32[]{:S(2)}) copy-start(bf16[512,16,64]{0,2,1:T(8,128)(2,1)} %copy-done.13) | copy-start | bytes 3145732
  429.1 47.9 %copy-start.16 = (bf16[512,16,64]{0,2,1:T(8,128)(2,1)S(1)}, bf16[512,16,64]{0,2,1:T(8,128)(2,1)}, u32[]{:S(2)}) copy-start(bf16[512,16,64]{0,2,1:T(8,128)(2,1)} %copy-done.15) | copy-start | bytes 3145732
  439.8 44.9 %copy-start.27 = (f32[512]{0:T(512)S(1)}, f32[512]{0:T(512)}, u32[]{:S(2)}) copy-start(f32[512]{0:T(512)} %copy-done.26) | copy-start | bytes 6148
  477.0 8.7 %copy-start.20 = (bf16[512,1024]{1,0:T(8,128)(2,1)S(1)}, bf16[512,1024]{1,0:T(8,128)(2,1)}, u32[]{:S(2)}) copy-start(bf16[512,1024]{1,0:T(8,128)(2,1)} %param.25) | copy-start | bytes 3145732
  523.5 10.8 %copy-start.12 = (bf16[512,16,64]{0,2,1:T(8,128)(2,1)S(1)}, bf16[512,16,64]{0,2,1:T(8,128)(2,1)}, u32[]{:S(2)}) copy-start(bf16[512,16,64]{0,2,1:T(8,128)(2,1)} %copy-done.11) | copy-start | bytes 3145732
  523.5 10.8 %copy-start.32 = (bf16[1024,1024]{1,0:T(8,128)(2,1)S(1)}, bf16[1024,1024]{1,0:T(8,128)(2,1)}, u32[]{:S(2)}) copy-start(bf16[1024,1024]{1,0:T(8,128)(2,1)} %all-gather.8.cloned.1.call-done) | copy-start | bytes 6291460
  692.6 5.7 copy-start.6
  698.3 2.5 copy-start.5
Sparse Core Ops, SparseCore 0:
  9.6 36.6 all-gather.7
  47.8 75.1 all-gather.9
  124.6 58.5 all-gather.11
  187.1 32.8 reduce-scatter.6
  222.3 58.8 reduce-scatter.4
  283.6 71.3 reduce-scatter.10
  357.6 71.3 reduce-scatter.8
  430.6 46.3 all-gather.13
  481.5 211.0 all-reduce.8
